TPU v7x, 256 devices: a whole 4x4x8 slice. The times are simulated.
256 devices in a mesh: gal: 8 (over y, core), pix: 32 (over x, z).
Axes of the slice: x: 4, y: 4, z: 8, core: 2. Of those that a mesh axis runs over, the one named last changes fastest.
Arguments:
- observed: float32 [32768, 4096], P('pix', 'gal'), may hold values from -6 to 6
- sparse_init: float32 [32768, 4096], P('pix', 'gal'), may hold values from -4 to 4
- dual_init: float32 [32768, 4096], P('pix', 'gal'), may hold values from -4 to 4
- right_init: float32 [64, 4096], P(None, 'gal'), may hold values from -0.09375 to 0.09375
Outputs:
- sparse: float32 [32768, 4096], P('pix', 'gal')
- dual: float32 [32768, 4096], P('pix', 'gal')
- left: float32 [64, 32768], P(None, 'pix')
- right: float32 [64, 4096], P(None, 'gal')
All inputs are finite; a program needn't handle non-finite values.
Results may differ from a plain program's by a relative error of at most 0.0003.
Values sent between devices are 32-bit elements; how exact they have to be, the bound alone decides.
A program may use at most 64 MiB of HBM per device.

v0:
```python
import jax
import jax.numpy as jnp
from jax import lax
from jax.sharding import PartitionSpec as P

ITERS = 2


MU = 1.25
TAU = 0.6 / 1.25
HIGH = lax.Precision.HIGHEST


def gram_of(panel):
    return lax.dot_general(panel, panel, (((1,), (1,)), ((), ())), precision=HIGH)


def orth_with(panel, gram):
    factor = jnp.linalg.cholesky(gram)
    return jax.scipy.linalg.solve_triangular(factor, panel, lower=True)


def shrink(values):
    return jnp.sign(values) * jnp.maximum(jnp.abs(values) - TAU, 0.0)


def per_device(observed, sparse_init, dual_init, right_init):
    sparse, dual, right = (sparse_init, dual_init, right_init)
    left = None
    for step in range(ITERS):
        target = observed - sparse + dual / MU
        partial_left = lax.dot_general(right, target, (((1,), (1,)), ((), ())), precision=HIGH)
        panel = lax.psum(partial_left, "gal")
        gram_left = lax.psum(gram_of(panel), "pix")
        left = orth_with(panel, gram_left)
        partial_wide = jnp.dot(left, target, precision=HIGH)
        wide = lax.psum(partial_wide, "pix")
        lowrank = lax.dot_general(left, wide, (((0,), (0,)), ((), ())), precision=HIGH)
        sparse = shrink(observed - lowrank + dual / MU)
        dual = dual + MU * (observed - lowrank - sparse)
        gram_right = lax.psum(gram_of(wide), "gal")
        right = orth_with(wide, gram_right)
    return (sparse, dual, left, right)


def solution(mesh):
    return jax.shard_map(
        per_device,
        mesh=mesh,
        in_specs=(P("pix", "gal"), P("pix", "gal"), P("pix", "gal"), P(None, "gal")),
        out_specs=(P("pix", "gal"), P("pix", "gal"), P(None, "pix"), P(None, "gal")),
        check_vma=False,
    )
```

profile of v0, /device:TPU:1, one launch (start us, length us, event | category | flops | bytes accessed | tf_op | source)
XLA Modules:
  0.0 834.7 jit_solution(9455242366928281128)
XLA Ops:
  7.2 0.8 copy-done
  8.1 6.0 convolution_bitcast_fusion
  14.2 67.2 %all-reduce.5.cloned.1.call-done = f32[64,1024]{1,0:T(8,128)} async-done(((f32[64,1024]{1,0:T(8,128)}), f32[64,1024]{1,0:T(8,128)}) %all-reduce.5.cloned.1.call-update) | async-done | bytes 262160 | tf_op jit(solution)/shard_map/psum | solution.py:33
  81.4 1.4 fusion.21
  82.8 115.7 %psum.57 = f32[64,64]{0,1:T(8,128)S(1)} all-reduce(f32[64,64]{0,1:T(8,128)S(1)} %fusion.21), channel_id=1, replica_groups=mesh['gal'=8,'pix'=32] {'pix'}, use_global_device_ids=true, to_apply=%region_1.0 | all-reduce | flops 4096 | bytes 32768 | tf_op jit(solution)/shard_map/psum | solution.py:34
  198.6 5.8 cholesky.74
  205.1 0.7 fusion
  205.8 4.9 custom-call.10
  210.7 1.4 fusion.13
  212.1 4.4 fusion.20
  216.6 159.0 %all-reduce.7.cloned.1.call-done = f32[64,512]{1,0:T(8,128)} async-done(((f32[64,512]{1,0:T(8,128)}), f32[64,512]{1,0:T(8,128)}) %all-reduce.7.cloned.1.call-update) | async-done | bytes 131088 | tf_op jit(solution)/shard_map/psum | solution.py:37
  375.6 1.2 fusion.22
  376.8 25.2 %psum.59 = f32[64,64]{0,1:T(8,128)S(1)} all-reduce(f32[64,64]{0,1:T(8,128)S(1)} %fusion.22), channel_id=1, replica_groups=mesh['gal'=8,'pix'=32] {'gal'}, use_global_device_ids=true, to_apply=%region_5.8 | all-reduce | flops 4096 | bytes 32768 | tf_op jit(solution)/shard_map/psum | solution.py:41
  402.1 5.8 cholesky.85
  409.3 4.9 custom-call.11
  414.2 6.1 subtract_add_fusion
  420.7 1.0 copy-done.2
  421.7 2.8 fusion.23
  424.6 62.2 %all-reduce.9.cloned.1.call-done = f32[64,1024]{1,0:T(8,128)} async-done(((f32[64,1024]{1,0:T(8,128)}), f32[64,1024]{1,0:T(8,128)}) %all-reduce.9.cloned.1.call-update) | async-done | bytes 262160 | tf_op jit(solution)/shard_map/psum | solution.py:33
  486.8 1.4 fusion.24
  488.2 115.7 %psum.61 = f32[64,64]{0,1:T(8,128)S(1)} all-reduce(f32[64,64]{0,1:T(8,128)S(1)} %fusion.24), channel_id=1, replica_groups=mesh['gal'=8,'pix'=32] {'pix'}, use_global_device_ids=true, to_apply=%region_7.0 | all-reduce | flops 4096 | bytes 32768 | tf_op jit(solution)/shard_map/psum | solution.py:34
  604.0 5.8 cholesky.96
  611.2 4.9 custom-call.12
  616.0 1.4 fusion.7
  617.4 3.7 fusion.25
  621.2 159.1 %all-reduce.11.cloned.1.call-done = f32[64,512]{1,0:T(8,128)} async-done(((f32[64,512]{1,0:T(8,128)}), f32[64,512]{1,0:T(8,128)}) %all-reduce.11.cloned.1.call-update) | async-done | bytes 131088 | tf_op jit(solution)/shard_map/psum | solution.py:37
  780.3 1.2 fusion.26
  781.5 25.2 %psum.63 = f32[64,64]{0,1:T(8,128)S(1)} all-reduce(f32[64,64]{0,1:T(8,128)S(1)} %fusion.26), channel_id=1, replica_groups=mesh['gal'=8,'pix'=32] {'gal'}, use_global_device_ids=true, to_apply=%region_9.13 | all-reduce | flops 4096 | bytes 32768 | tf_op jit(solution)/shard_map/psum | solution.py:41
  806.9 5.8 cholesky.107
  814.1 4.9 custom-call.13
  819.0 8.2 multiply_add_fusion
  827.2 1.0 fusion.4
  (38 shorter events, 5.6 us)
Async XLA Ops:
  7.2 0.9 copy-start
  7.2 74.2 %all-reduce.5.cloned.1.call-start = ((), (), s32[]{:S(2)}) async-start(), calls=%async_computation | async-start | bytes 524288 | tf_op jit(solution)/shard_map/psum | solution.py:33
  8.1 204.0 %copy-start.1 = (f32[1024,512]{1,0:T(8,128)S(1)}, f32[1024,512]{1,0:T(8,128)}, u32[]{:S(2)}) copy-start(f32[1024,512]{1,0:T(8,128)} %param.11) | copy-start | bytes 6291460
  14.1 361.5 %all-reduce.7.cloned.1.call-start = ((), (), s32[]{:S(2)}) async-start(), calls=%async_computation.1 | async-start | bytes 262144 | tf_op jit(solution)/shard_map/psum | solution.py:37
  216.5 270.3 %all-reduce.9.cloned.1.call-start = ((), (), s32[]{:S(2)}) async-start(), calls=%async_computation.2 | async-start | bytes 524288 | tf_op jit(solution)/shard_map/psum | solution.py:33
  414.2 6.2 copy-start.4
  420.4 1.3 copy-start.2
  424.6 355.7 %all-reduce.11.cloned.1.call-start = ((), (), s32[]{:S(2)}) async-start(), calls=%async_computation.3 | async-start | bytes 262144 | tf_op jit(solution)/shard_map/psum | solution.py:37
  617.4 209.8 %copy-start.3 = (f32[64,1024]{1,0:T(8,128)}, f32[64,1024]{1,0:T(8,128)S(1)}, u32[]{:S(2)}) copy-start(f32[64,1024]{1,0:T(8,128)S(1)} %fusion.7) | copy-start | bytes 786436
  819.0 8.3 copy-start.5
Sparse Core Ops, SparseCore 0:
  14.3 67.1 all-reduce.4
  216.6 158.9 all-reduce.6
  424.7 62.0 all-reduce.8
  621.3 158.9 all-reduce.10
where the time goes:
time: 837 us; the launch traced here: 835 us
  waiting for transfers between devices  448 us (54%)
  blocking collectives  282 us (34%)
  other arithmetic  48.3 us (6%)
  matrix products  40.7 us (5%)
  between operations  14 us (2%)
    psum x2, waiting for transfers between devices, per_device(): wide = lax.psum(partial_wide, 'pix')  318 us
    psum x2, blocking collectives, per_device(): gram_left = lax.psum(gram_of(panel), 'pix')  231 us
    psum x2, waiting for transfers between devices, per_device(): panel = lax.psum(partial_left, 'gal')  129 us
    psum x2, blocking collectives, per_device(): gram_right = lax.psum(gram_of(wide), 'gal')  50.5 us
    another operation x12, other arithmetic, orth_with(): factor = jnp.linalg.cholesky(gram)  26.1 us
    another operation x8, other arithmetic, orth_with(): return jax.scipy.linalg.solve_triangular(factor, panel, lower=True)  22.2 us
  transfers between devices with their start and end apart: 4, of which 4 were waited for; matrix products, arithmetic and copies ran while one was open for 0% of the time, Pallas kernels for 0%

commit v1 on v0

v1 whole, which is shorter than its diff:
```python
import functools

import jax
import jax.numpy as jnp
from jax import lax
from jax.experimental import pallas as pl
from jax.experimental.pallas import tpu as pltpu
from jax.sharding import PartitionSpec as P

MU = 1.25
TAU = 0.6 / 1.25
INV_MU = 1.0 / MU
HIGH = lax.Precision.HIGHEST
MESH = pl.DeviceIdType.MESH
F32 = jnp.float32
BF16 = jnp.bfloat16

NG = 8
NZ = 8
NX = 4
R = 64
ROWS = 1024
COLS = 512
GB = ROWS // NG
RB = R // NZ
CHUNK = 256
NCH = ROWS // CHUNK

PRS, PAG, WRS, WX, WAG, KRS, KX, KAG, GAR = range(9)

NN = (((1,), (0,)), ((), ()))
NT = (((1,), (1,)), ((), ()))
TN = (((0,), (0,)), ((), ()))


def split(value):
    high = value.astype(BF16)
    return high, (value - high.astype(F32)).astype(BF16)


def mm(a, b, dims):
    return lax.dot_general(a, b, dims, preferred_element_type=F32)


def mm_high(a, b, dims):
    return lax.dot_general(a, b, dims, precision=HIGH, preferred_element_type=F32)


def inverse_factor(gram2):
    lane = lax.broadcasted_iota(jnp.int32, (8, 128), 1)
    sub = lax.broadcasted_iota(jnp.int32, (8, 128), 0)
    tiles = []
    for b in range(8):
        eye = jnp.where(lane == sub + 8 * b, 1.0, 0.0)
        tiles.append(jnp.where(lane < R, eye, gram2[8 * b : 8 * b + 8, :]))
    for j in range(R):
        t = j // 8
        pivot = tiles[t][j % 8 : j % 8 + 1, :]
        scaled = pivot * (1.0 / pivot[:, R + j : R + j + 1])
        for b in range(t, 8):
            column = tiles[b][:, R + j : R + j + 1]
            update = column * scaled
            if b == t:
                update = jnp.where(sub > j % 8, update, 0.0)
            tiles[b] = tiles[b] - update
    out = []
    for b in range(8):
        diag = jnp.sum(jnp.where(lane == sub + 8 * b + R, tiles[b], 0.0), axis=1, keepdims=True)
        out.append(tiles[b] * (1.0 / jnp.sqrt(diag)))
    return jnp.concatenate(out, axis=0)[:, :R]


def kernel(
    obs_hbm, sp_hbm, du_hbm, right_ref, x_hbm, left_ref, right_out,
    obs, work, dual, thi, tlo, lstk,
    part, prs, psrc, panel, wpart, wrs, wsrc, wx, wres, wraw,
    kpart, krs, ksrc, kx, kres, kraw, gsrc, gall,
    load_sem, store_sem, send_sem, recv_sem,
):
    g = lax.axis_index("gal")
    pix = lax.axis_index("pix")
    z = lax.rem(pix, NZ)
    x = lax.div(pix, NZ)

    def gal_peer(t):
        return {"gal": t, "pix": pix}

    def z_peer(t):
        return {"gal": g, "pix": x * NZ + t}

    def x_peer(t):
        return {"gal": g, "pix": t * NZ + z}

    def loads(ch):
        rows = pl.ds(ch * CHUNK, CHUNK)
        return [
            pltpu.make_async_copy(src.at[rows, :], dst.at[rows, :], load_sem.at[i, ch])
            for i, (src, dst) in enumerate(((obs_hbm, obs), (sp_hbm, work), (du_hbm, dual)))
        ]

    barrier = pltpu.get_barrier_semaphore()
    for n, me, peer in ((NG, g, gal_peer), (NZ, z, z_peer), (NX, x, x_peer)):
        for k in range(1, n):
            pl.semaphore_signal(barrier, inc=1, device_id=peer(lax.rem(me + k, n)), device_id_type=MESH)
    for ch in range(NCH):
        for copy in loads(ch):
            copy.start()

    def send(it, kind, src, dst, peer):
        pltpu.make_async_remote_copy(
            src_ref=src, dst_ref=dst, send_sem=send_sem.at[it, kind], recv_sem=recv_sem.at[it, kind],
            device_id=peer, device_id_type=MESH,
        ).start()

    def spread(it, kind, n, me, peer, src_of, dst):
        order = sorted(range(1, n), key=lambda k: -min(k, n - k))
        for k in order:
            t = lax.rem(me + k, n)
            send(it, kind, src_of(t), dst.at[it, me], peer(t))

    def arrived(it, kind, n, dst):
        view = dst.at[it, pl.ds(0, n - 1)]
        pltpu.make_async_copy(view, view, recv_sem.at[it, kind]).wait()

    def sent(it, kind, n, dst):
        view = dst.at[it, pl.ds(0, n - 1)]
        pltpu.make_async_copy(view, view, send_sem.at[it, kind]).wait()

    def total(buf, it, n):
        acc = buf[it, 0]
        for i in range(1, n):
            acc = acc + buf[it, i]
        return acc

    def panel_chunk(it, ch, r2, r_high, t_high, t_low):
        both = mm(r2, t_high, NT)
        p = both[:R] + both[R:] + mm(r_high, t_low, NT)
        for i in range(CHUNK // GB):
            d = ch * (CHUNK // GB) + i
            part[it, d] = p[:, i * GB : (i + 1) * GB]

            @pl.when(g != d)
            def _():
                send(it, PRS, part.at[it, d], prs.at[it, g], gal_peer(d))

    def finish_panel(it):
        prs[it, g] = part[it, g]

    r_high, r_low = split(right_ref[...])
    r2 = jnp.concatenate([r_high, r_low], axis=0)
    for ch in range(NCH):
        rows = pl.ds(ch * CHUNK, CHUNK)
        for copy in loads(ch):
            copy.wait()
        c = dual[rows, :] * INV_MU
        dual[rows, :] = c
        t_high, t_low = split(obs[rows, :] - work[rows, :] + c)
        thi[rows, :] = t_high
        tlo[rows, :] = t_low
        if ch == 0:
            pl.semaphore_wait(barrier, NG + NZ + NX - 3)
        panel_chunk(0, ch, r2, r_high, t_high, t_low)
    finish_panel(0)

    inv_right = None
    for it in range(2):
        if it == 1:
            arrived(0, GAR, NG, gall)
            packed = total(gall, 0, NG)
            inv_right = inverse_factor(jnp.concatenate([pltpu.roll(packed, R, 1), packed], axis=0))
        arrived(it, PRS, NG, prs)
        mine = total(prs, it, NG)
        if it == 1:
            mine = mm_high(inv_right, mine, NN)
        psrc[it] = mine
        spread(it, PAG, NG, g, gal_peer, lambda t: psrc.at[it], panel)
        panel[it, g] = mine
        arrived(it, PAG, NG, panel)
        whole = jnp.concatenate([panel[it, i] for i in range(NG)], axis=1)

        gram = mm_high(whole, jnp.concatenate([whole, whole], axis=0), NT)
        for d in range(NZ):
            kpart[it, d] = gram[d * RB : (d + 1) * RB]
        spread(it, KRS, NZ, z, z_peer, lambda t: kpart.at[it, t], krs)
        krs[it, z] = kpart[it, z]

        p_high, p_low = split(whole)
        p2 = jnp.concatenate([p_high, p_low], axis=0)
        both = mm(p2, thi[...], NN)
        raw = both[:R] + both[R:] + mm(p_high, tlo[...], NN)
        for d in range(NZ):
            wpart[it, d] = raw[d * RB : (d + 1) * RB]
        spread(it, WRS, NZ, z, z_peer, lambda t: wpart.at[it, t], wrs)
        wrs[it, z] = wpart[it, z]

        arrived(it, KRS, NZ, krs)
        mine = total(krs, it, NZ)
        ksrc[it] = mine
        spread(it, KX, NX, x, x_peer, lambda t: ksrc.at[it], kx)
        kx[it, x] = mine
        arrived(it, KX, NX, kx)
        mine = total(kx, it, NX)
        kres[it] = mine
        spread(it, KAG, NZ, z, z_peer, lambda t: kres.at[it], kraw)
        kraw[it, z] = mine

        arrived(it, WRS, NZ, wrs)
        mine = total(wrs, it, NZ)
        wsrc[it] = mine
        spread(it, WX, NX, x, x_peer, lambda t: wsrc.at[it], wx)
        wx[it, x] = mine
        arrived(it, WX, NX, wx)
        mine = total(wx, it, NX)
        wres[it] = mine
        spread(it, WAG, NZ, z, z_peer, lambda t: wres.at[it], wraw)
        wraw[it, z] = mine

        arrived(it, KAG, NZ, kraw)
        inv_left = inverse_factor(jnp.concatenate([kraw[it, i] for i in range(NZ)], axis=0))
        left = mm_high(inv_left, whole, NN)
        l_high, l_low = split(left)
        lstk[0:R, :] = l_high
        lstk[R : 2 * R, :] = l_high
        lstk[2 * R : 3 * R, :] = l_low
        if it == 1:
            left_ref[...] = left

        arrived(it, WAG, NZ, wraw)
        wide = mm_high(inv_left, jnp.concatenate([wraw[it, i] for i in range(NZ)], axis=0), NN)
        w_high, w_low = split(wide)
        wstk = jnp.concatenate([w_high, w_low, w_high], axis=0)

        gram = mm_high(wide, jnp.concatenate([wide, wide], axis=0), NT)
        lane = lax.broadcasted_iota(jnp.int32, (R // 2, 128), 1)
        packed = jnp.where(lane < R, gram[: R // 2], gram[R // 2 :])
        gsrc[it] = packed
        spread(it, GAR, NG, g, gal_peer, lambda t: gsrc.at[it], gall)
        gall[it, g] = packed

        r2 = jnp.concatenate([w_high, w_low], axis=0)
        for ch in range(NCH):
            rows = pl.ds(ch * CHUNK, CHUNK)
            low = mm(lstk[:, rows], wstk, TN)
            c = dual[rows, :]
            v = obs[rows, :] + c - low
            if it == 0:
                clipped = jnp.minimum(jnp.maximum(v, -TAU), TAU)
                dual[rows, :] = clipped
                t_high, t_low = split(low - c + (clipped + clipped))
                thi[rows, :] = t_high
                tlo[rows, :] = t_low
                panel_chunk(1, ch, r2, w_high, t_high, t_low)
            else:
                work[rows, :] = v
                pltpu.make_async_copy(work.at[rows, :], x_hbm.at[rows, :], store_sem.at[ch]).start()
        if it == 0:
            finish_panel(1)
        else:
            arrived(1, GAR, NG, gall)
            packed = total(gall, 1, NG)
            inv_right = inverse_factor(jnp.concatenate([pltpu.roll(packed, R, 1), packed], axis=0))
            right_out[...] = mm_high(inv_right, wide, NN)

    for ch in range(NCH):
        rows = pl.ds(ch * CHUNK, CHUNK)
        pltpu.make_async_copy(work.at[rows, :], x_hbm.at[rows, :], store_sem.at[ch]).wait()
    for it in range(2):
        for kind, n, buf in (
            (PRS, NG, prs), (PAG, NG, panel), (WRS, NZ, wrs), (WX, NX, wx), (WAG, NZ, wraw),
            (KRS, NZ, krs), (KX, NX, kx), (KAG, NZ, kraw), (GAR, NG, gall),
        ):
            sent(it, kind, n, buf)


def per_device(observed, sparse_init, dual_init, right_init):
    hbm = pl.BlockSpec(memory_space=pl.ANY)
    vmem = pl.BlockSpec(memory_space=pltpu.VMEM)
    shape = (ROWS, COLS)
    x, left, right = pl.pallas_call(
        kernel,
        out_shape=(
            jax.ShapeDtypeStruct(shape, F32),
            jax.ShapeDtypeStruct((R, ROWS), F32),
            jax.ShapeDtypeStruct((R, COLS), F32),
        ),
        in_specs=[hbm, hbm, hbm, vmem],
        out_specs=(hbm, vmem, vmem),
        scratch_shapes=[
            pltpu.VMEM(shape, F32),
            pltpu.VMEM(shape, F32),
            pltpu.VMEM(shape, F32),
            pltpu.VMEM(shape, BF16),
            pltpu.VMEM(shape, BF16),
            pltpu.VMEM((3 * R, ROWS), BF16),
            pltpu.VMEM((2, NG, R, GB), F32),
            pltpu.VMEM((2, NG, R, GB), F32),
            pltpu.VMEM((2, R, GB), F32),
            pltpu.VMEM((2, NG, R, GB), F32),
            pltpu.VMEM((2, NZ, RB, COLS), F32),
            pltpu.VMEM((2, NZ, RB, COLS), F32),
            pltpu.VMEM((2, RB, COLS), F32),
            pltpu.VMEM((2, NX, RB, COLS), F32),
            pltpu.VMEM((2, RB, COLS), F32),
            pltpu.VMEM((2, NZ, RB, COLS), F32),
            pltpu.VMEM((2, NZ, RB, 2 * R), F32),
            pltpu.VMEM((2, NZ, RB, 2 * R), F32),
            pltpu.VMEM((2, RB, 2 * R), F32),
            pltpu.VMEM((2, NX, RB, 2 * R), F32),
            pltpu.VMEM((2, RB, 2 * R), F32),
            pltpu.VMEM((2, NZ, RB, 2 * R), F32),
            pltpu.VMEM((2, R // 2, 2 * R), F32),
            pltpu.VMEM((2, NG, R // 2, 2 * R), F32),
            pltpu.SemaphoreType.DMA((3, NCH)),
            pltpu.SemaphoreType.DMA((NCH,)),
            pltpu.SemaphoreType.DMA((2, 9)),
            pltpu.SemaphoreType.DMA((2, 9)),
        ],
        compiler_params=pltpu.CompilerParams(collective_id=0, has_side_effects=True, vmem_limit_bytes=48 << 20),
        name="pursuit",
    )(observed, sparse_init, dual_init, right_init)
    clipped = jnp.minimum(jnp.maximum(x, -TAU), TAU)
    return x - clipped, MU * clipped, left, right


def solution(mesh):
    return jax.shard_map(
        per_device,
        mesh=mesh,
        in_specs=(P("pix", "gal"), P("pix", "gal"), P("pix", "gal"), P(None, "gal")),
        out_specs=(P("pix", "gal"), P("pix", "gal"), P(None, "pix"), P(None, "gal")),
        check_vma=False,
    )
```

time: 837 us -> 92.5 us (0.11)
  waiting for transfers between devices: 448 us -> 0 us
  blocking collectives: 282 us -> 0 us
  Pallas kernels: 0 us -> 85.2 us
  other arithmetic: 48.3 us -> 2.68 us
  matrix products: 40.7 us -> 0 us
  between operations: 14 us -> 0.65 us
    psum x4 -> x0, waiting for transfers between devices: 448 us -> none  [the longest x2 318 us: per_device(): wide = lax.psum(partial_wide, 'pix')]
    psum x4 -> x0, blocking collectives: 282 us -> none  [the longest x2 231 us: per_device(): gram_left = lax.psum(gram_of(panel), 'pix')]
    pallas_call x0 -> x1, Pallas kernels: none -> 85.2 us  [per_device(): pl.pallas_call(kernel, out_shape=(jax.ShapeDtypeStruct(shape, F32), jax.S...]
    another operation x20 -> x0, other arithmetic: 48.3 us -> none  [the longest x12 26.1 us: orth_with(): factor = jnp.linalg.cholesky(gram)]
    dot_general x10 -> x0, matrix products: 36.7 us -> none  [the longest x2 14.4 us: per_device(): lax.dot_general(left, wide, (((0,), (0,)), ((), ())), precision=HIGH)]
  transfers between devices with their start and end apart: 4 -> 0, of which waited for: 4 -> 0; matrix products, arithmetic and copies ran while one was open for 0% -> 0% of each run, Pallas kernels for 0% -> 0%
where the time goes in v1:
time: 92.5 us; the launch traced here: 92.4 us
  Pallas kernels  85.2 us (92%)
  local copies, waits for them, and re-layouts  3.84 us (4%)
  other arithmetic  2.68 us (3%)
    pallas_call x1, Pallas kernels, per_device(): pl.pallas_call(kernel, out_shape=(jax.ShapeDtypeStruct(shape, F32), jax.S...  85.2 us
    unnamed x6, local copies, waits for them, and re-layouts  3.84 us
    mul x1, other arithmetic, per_device(): return (x - clipped, MU * clipped, left, right)  2.68 us

profile of v1, /device:TPU:1, one launch (start us, length us, event | category | flops | bytes accessed | tf_op | source)
XLA Modules:
  0.0 92.4 jit_solution(8493274144212739624)
XLA Ops:
  0.6 0.0 copy-start
  0.6 1.6 %copy-done = f32[1024,512]{1,0:T(8,128)S(1)} copy-done((f32[1024,512]{1,0:T(8,128)S(1)}, f32[1024,512]{1,0:T(8,128)}, u32[]{:S(2)}) %copy-start) | copy-done | bytes 2097176
  2.2 0.0 copy-start.1
  2.2 0.9 copy-done.1
  3.1 85.2 %pursuit.1 = (f32[1024,512]{1,0:T(8,128)S(1)}, f32[64,1024]{1,0:T(8,128)S(1)}, f32[64,512]{1,0:T(8,128)S(1)}) custom-call(f32[1024,512]{1,0:T(8,128)S(1)} %copy-done, f32[1024,512]{1,0:T(8,128)} %sp_hbm.1, f32[1024,512]{1,0:T(8,128)} %du_hbm.1, f32[64,512]{1,0:T(8,128)S(1)} %copy-done.1), custom_call_target="tpu_custom_call" | custom-call | tf_op jit(solution)/shard_map/pursuit/pallas_call | solution.py:279
  88.3 2.7 %clamp_multiply_fusion = (f32[1024,512]{1,0:T(8,128)}, f32[1024,512]{1,0:T(8,128)}) fusion(f32[1024,512]{1,0:T(8,128)S(1)} %get-tuple-element.7), kind=kLoop, calls=%fused_computation | loop fusion | flops 1572864 | bytes 6291456 | tf_op jit(solution)/shard_map/mul | solution.py:322
  91.0 0.7 copy.10
  91.7 0.7 copy.11
Async XLA Ops:
  0.6 1.6 %copy-start = (f32[1024,512]{1,0:T(8,128)S(1)}, f32[1024,512]{1,0:T(8,128)}, u32[]{:S(2)}) copy-start(f32[1024,512]{1,0:T(8,128)} %obs_hbm.1) | copy-start | bytes 6291460
  2.2 0.9 copy-start.1

commit v2 on v0

v2 whole, which is shorter than its diff:
```python
import contextlib

import jax
import jax.numpy as jnp
from jax import lax
from jax.experimental import pallas as pl
from jax.experimental.pallas import tpu as pltpu
from jax.sharding import PartitionSpec as P

MU = 1.25
TAU = 0.6 / 1.25
INV_MU = 1.0 / MU
HIGH = lax.Precision.HIGHEST
MESH = pl.DeviceIdType.MESH
F32 = jnp.float32
BF16 = jnp.bfloat16

NY = 4
NG = 8
NZ = 8
NX = 4
NP = NZ * NX
R = 64
ROWS = 1024
COLS = 512
GB = ROWS // NG
RB = 8
LB = 128
CHUNK = ROWS // NY
ORDER = (2, 1, 3, 0)

PIX_ORDER = sorted(
    ((i, j) for i in range(NX) for j in range(NZ) if i or j), key=lambda k: -(min(k[0], NX - k[0]) + min(k[1], NZ - k[1]))
)

PRS, PAG, WRS, WAG, KZ, KX, KAG, GAR = range(8)

NN = (((1,), (0,)), ((), ()))
NT = (((1,), (1,)), ((), ()))
TN = (((0,), (0,)), ((), ()))


def split(value):
    high = value.astype(BF16)
    return high, (value - high.astype(F32)).astype(BF16)


def mm(a, b, dims):
    return lax.dot_general(a, b, dims, preferred_element_type=F32)


def mm_high(a, b, dims):
    return lax.dot_general(a, b, dims, precision=HIGH, preferred_element_type=F32)


def clip(value):
    return jnp.minimum(jnp.maximum(value, -TAU), TAU)


def inverse_factor(gram2):
    tile = (8, 128)
    lane = lax.broadcasted_iota(jnp.int32, tile, 1)
    sub = lax.broadcasted_iota(jnp.int32, tile, 0)
    tiles, out = [], []
    for b in range(8):
        eye = jnp.where(lane == sub + 8 * b, 1.0, 0.0)
        tiles.append(jnp.where(lane < R, eye, gram2[8 * b : 8 * b + 8, :]))
        out.append(None)

    def column(value, k):
        return jnp.broadcast_to(value[:, R + k : R + k + 1], tile)

    for j in range(0, R, 4):
        t, o = j // 8, j % 8
        r0, r1, r2, r3 = (jnp.broadcast_to(tiles[t][o + p : o + p + 1, :], tile) for p in range(4))
        a00, a01, b00, b01 = (column(r0, j + q) for q in range(4))
        a11, b10, b11 = (column(r1, j + q) for q in range(1, 4))
        d00, d01 = (column(r2, j + q) for q in range(2, 4))
        d11 = column(r3, j + 3)
        det = a00 * a11 - a01 * a01
        inv = 1.0 / det
        n00, n01, n11 = a11 * inv, -(a01 * inv), a00 * inv
        x00, x01 = n00 * b00 + n01 * b10, n00 * b01 + n01 * b11
        x10, x11 = n01 * b00 + n11 * b10, n01 * b01 + n11 * b11
        s00 = d00 - (b00 * x00 + b10 * x10)
        s01 = d01 - (b00 * x01 + b10 * x11)
        s11 = d11 - (b01 * x01 + b11 * x11)
        sdet = s00 * s11 - s01 * s01
        sinv = 1.0 / sdet
        m00, m01, m11 = s11 * sinv, -(s01 * sinv), s00 * sinv
        u2 = r2 - (x00 * r0 + x10 * r1)
        u3 = r3 - (x01 * r0 + x11 * r1)
        if j + 4 < R:
            y2, y3 = m00 * u2 + m01 * u3, m01 * u2 + m11 * u3
            y0 = (n00 * r0 + n01 * r1) - (x00 * y2 + x01 * y3)
            y1 = (n01 * r0 + n11 * r1) - (x10 * y2 + x11 * y3)
            for b in range(t if o == 0 else t + 1, 8):
                c0, c1, c2, c3 = (column(tiles[b], j + p) for p in range(4))
                update = (c0 * y0 + c1 * y1) + (c2 * y2 + c3 * y3)
                if b == t:
                    update = jnp.where(sub >= 4, update, 0.0)
                tiles[b] = tiles[b] - update
        f0 = r0 * (1.0 / jnp.sqrt(a00))
        f1 = (r1 - (a01 / a00) * r0) * (1.0 / jnp.sqrt(det / a00))
        f2 = u2 * (1.0 / jnp.sqrt(s00))
        f3 = (u3 - (s01 / s00) * u2) * (1.0 / jnp.sqrt(sdet / s00))
        quad = jnp.where(sub == o, f0, jnp.where(sub == o + 1, f1, jnp.where(sub == o + 2, f2, f3)))
        out[t] = quad if o == 0 else jnp.where(sub < 4, out[t], quad)
    return jnp.concatenate(out, axis=0)[:, :R]


def factor_of(packed):
    return inverse_factor(jnp.concatenate([pltpu.roll(packed, R, 1), packed], axis=0))


def scope(name):
    return contextlib.nullcontext()


def kernel(
    obs_hbm, sp_hbm, du_hbm, right_hbm, sparse_out, dual_out, left_ref, wide_ref, gram_ref,
    right_ref, obs, work, dual, thi, tlo, lstk,
    part, prs, panel, normal, wpart, wrs, wraw, kz, kx, kraw, gall,
    load_sem, send_sem, recv_sem, near_sem, relay_sem,
):
    g = lax.axis_index("gal")
    pix = lax.axis_index("pix")
    y, core = lax.div(g, 2), lax.rem(g, 2)
    other = 1 - core
    z = lax.rem(pix, NZ)
    x = lax.div(pix, NZ)

    def gal_peer(t):
        return {"gal": t, "pix": pix}

    def z_peer(t):
        return {"gal": g, "pix": x * NZ + t}

    def x_peer(t):
        return {"gal": g, "pix": t * NZ + z}

    def pix_of(k):
        return lax.rem(x + k[0], NX) * NZ + lax.rem(z + k[1], NZ)

    def pix_peer(k):
        return {"gal": g, "pix": pix_of(k)}

    def chunk(k):
        return lax.rem(y + k, NY)

    def rows_of(k):
        return pl.ds(pl.multiple_of(chunk(k) * CHUNK, CHUNK), CHUNK)

    def loads(k):
        rows = rows_of(k)
        return [
            pltpu.make_async_copy(src.at[rows, :], dst.at[rows, :], load_sem.at[i, k])
            for i, (src, dst) in enumerate(((obs_hbm, obs), (sp_hbm, work), (du_hbm, dual)))
        ]

    barrier = pltpu.get_barrier_semaphore()
    for k in PIX_ORDER:
        pl.semaphore_signal(barrier, inc=1, device_id=pix_peer(k), device_id_type=MESH)
    for k in range(1, NG):
        pl.semaphore_signal(barrier, inc=1, device_id=gal_peer(lax.rem(g + k, NG)), device_id_type=MESH)
    load_right = pltpu.make_async_copy(right_hbm, right_ref, load_sem.at[3, 0])
    load_right.start()
    for k in ORDER:
        for copy in loads(k):
            copy.start()

    def send(it, kind, src, dst, peer, recv):
        pltpu.make_async_remote_copy(
            src_ref=src, dst_ref=dst, send_sem=send_sem.at[it, kind], recv_sem=recv,
            device_id=peer, device_id_type=MESH,
        ).start()

    def spread(it, kind, n, me, peer, src_of, dst):
        order = sorted(range(1, n), key=lambda k: -min(k, n - k))
        for k in order:
            t = lax.rem(me + k, n)
            send(it, kind, src_of(t), dst.at[it, me], peer(t), recv_sem.at[it, kind])

    def arrived(it, kind, n, dst):
        view = dst.at[it, pl.ds(0, n - 1)]
        pltpu.make_async_copy(view, view, recv_sem.at[it, kind]).wait()

    def landed(view, sem):
        pltpu.make_async_copy(view, view, sem).wait()

    def total(buf, it, n):
        acc = buf[it, 0]
        for i in range(1, n):
            acc = acc + buf[it, i]
        return acc

    def panel_chunk(it, k, r2, r_high, t_high, t_low):
        both = mm(r2, t_high, NT)
        p = both[:R] + both[R:] + mm(r_high, t_low, NT)
        first = 2 * chunk(k)
        part[it, first] = p[:, :GB]
        part[it, first + 1] = p[:, GB:]

    def send_chunk(it, k):
        first = 2 * chunk(k)
        if k == 0:
            send(it, PRS, part.at[it, 2 * y + other], prs.at[it, g], gal_peer(2 * y + other), recv_sem.at[it, PRS])
            prs[it, g] = part[it, g]
        else:
            for d in (first, first + 1):
                send(it, PRS, part.at[it, d], prs.at[it, g], gal_peer(d), recv_sem.at[it, PRS])

    with scope("load_right"):
        load_right.wait()
        r_high, r_low = split(right_ref[...])
        r2 = jnp.concatenate([r_high, r_low], axis=0)
    for k in ORDER:
        with scope("load"):
            for copy in loads(k):
                copy.wait()
        with scope("target"):
            rows = rows_of(k)
            c = dual[rows, :] * INV_MU
            dual[rows, :] = c
            t_high, t_low = split(obs[rows, :] - work[rows, :] + c)
            thi[rows, :] = t_high
            tlo[rows, :] = t_low
        with scope("panel"):
            panel_chunk(0, k, r2, r_high, t_high, t_low)
    with scope("barrier"):
        pl.semaphore_wait(barrier, NG + NP - 2)
    for k in ORDER:
        send_chunk(0, k)

    for it in range(2):
        with scope("w_prs"):
            arrived(it, PRS, NG, prs)
        with scope("pag_send"):
            panel[it, g] = total(prs, it, NG)
            own = panel.at[it, g]
            for k in (2, 1, 3):
                send(it, PAG, own, own, gal_peer(2 * chunk(k) + core), near_sem.at[it, NY - k])
            partner = gal_peer(2 * y + other)
            send(it, PAG, own, own, partner, near_sem.at[it, 0])
        if it == 1:
            with scope("w_gar"):
                arrived(0, GAR, NG, gall)
            with scope("chol_right"):
                inv_right = factor_of(total(gall, 0, NG))

        gram = raw = None
        for k in (0, 1, 3, 2):
            block = 2 * chunk(k)
            rows = rows_of(k)
            with scope("w_near"):
                landed(panel.at[it, block + other], near_sem.at[it, 0] if k == 0 else relay_sem.at[it, k])
            with scope("gram_left"):
                p = jnp.concatenate([panel[it, block], panel[it, block + 1]], axis=1)
                if it == 1:
                    p = mm_high(inv_right, p, NN)
                normal[:, rows] = p
                few = normal[pl.ds(pl.multiple_of(g * RB, RB), RB), rows]
                term = mm_high(few, jnp.concatenate([p, p], axis=0), NT)
                gram = term if gram is None else gram + term
                if k == 2:
                    kz[it, z] = gram
                    spread(it, KZ, NZ, z, z_peer, lambda t: kz.at[it, z], kz)
            with scope("raw_wide"):
                p_high, p_low = split(p)
                both = mm(jnp.concatenate([p_high, p_low], axis=0), thi[rows, :], NN)
                term = both[:R] + both[R:] + mm(p_high, tlo[rows, :], NN)
                raw = term if raw is None else raw + term
            if k == 0:
                with scope("w_relay"):
                    for kk in (1, 3, 2):
                        slot = panel.at[it, 2 * chunk(kk) + core]
                        landed(slot, near_sem.at[it, kk])
                        send(it, PAG, slot, slot, partner, relay_sem.at[it, kk])
        with scope("w_send"):
            for i in range(NX):
                for j in range(NZ):
                    wpart[it, i * NZ + j] = raw[j * RB : (j + 1) * RB, i * LB : (i + 1) * LB]
            for k in PIX_ORDER:
                send(it, WRS, wpart.at[it, pix_of(k)], wrs.at[it, pix], pix_peer(k), recv_sem.at[it, WRS])
            wrs[it, pix] = wpart[it, pix]

        with scope("w_kz"):
            arrived(it, KZ, NZ, kz)
        kx[it, x] = total(kz, it, NZ)
        spread(it, KX, NX, x, x_peer, lambda t: kx.at[it, x], kx)
        with scope("w_wrs"):
            arrived(it, WRS, NP, wrs)
        with scope("wag_send"):
            wraw[it, pix] = total(wrs, it, NP)
            own = wraw.at[it, pix]
            for k in PIX_ORDER:
                send(it, WAG, own, own, pix_peer(k), recv_sem.at[it, WAG])
        with scope("w_kx"):
            arrived(it, KX, NX, kx)
        kraw[it, g] = total(kx, it, NX)
        spread(it, KAG, NG, g, gal_peer, lambda t: kraw.at[it, g], kraw)

        with scope("w_kag"):
            arrived(it, KAG, NG, kraw)
        with scope("chol_left"):
            inv_left = inverse_factor(jnp.concatenate([kraw[it, i] for i in range(NG)], axis=0))
        with scope("left"):
            left = mm_high(inv_left, normal[...], NN)
            l_high, l_low = split(left)
            lstk[0:R, :] = l_high
            lstk[R : 2 * R, :] = l_high
            lstk[2 * R : 3 * R, :] = l_low
            if it == 1:
                left_ref[...] = left

        with scope("w_wag"):
            arrived(it, WAG, NP, wraw)
        with scope("wide"):
            columns = [jnp.concatenate([wraw[it, i * NZ + j] for j in range(NZ)], axis=0) for i in range(NX)]
            wide = mm_high(inv_left, jnp.concatenate(columns, axis=1), NN)
            w_high, w_low = split(wide)
            wstk = jnp.concatenate([w_high, w_low, w_high], axis=0)
            r2 = jnp.concatenate([w_high, w_low], axis=0)
        with scope("gram_right"):
            gram = mm_high(wide, jnp.concatenate([wide, wide], axis=0), NT)
            lane = lax.broadcasted_iota(jnp.int32, (R // 2, 128), 1)
            gall[it, g] = jnp.where(lane < R, gram[: R // 2], gram[R // 2 :])
            spread(it, GAR, NG, g, gal_peer, lambda t: gall.at[it, g], gall)
        for k in ORDER:
            with scope("update"):
                rows = rows_of(k)
                low = mm(lstk[:, rows], wstk, TN)
                c = dual[rows, :]
                if it == 0:
                    clipped = clip(obs[rows, :] + c - low)
                    dual[rows, :] = clipped
                    t_high, t_low = split(low - c + (clipped + clipped))
                    thi[rows, :] = t_high
                    tlo[rows, :] = t_low
                    panel_chunk(1, k, r2, w_high, t_high, t_low)
                    send_chunk(1, k)
                else:
                    v = obs[rows, :] + c - low
                    clipped = clip(v)
                    sparse_out[rows, :] = v - clipped
                    dual_out[rows, :] = MU * clipped

    wide_ref[...] = wide
    with scope("w_gar"):
        arrived(1, GAR, NG, gall)
    gram_ref[...] = total(gall, 1, NG)
    with scope("fin"):
        for it in range(2):
            for kind, n, buf in (
                (PRS, NG, prs), (PAG, NG, panel), (WRS, NP, wrs), (WAG, NP, wraw),
                (KZ, NZ, kz), (KX, NX, kx), (KAG, NG, kraw), (GAR, NG, gall),
            ):
                landed(buf.at[it, pl.ds(0, n - 1)], send_sem.at[it, kind])


def outputs(
    sparse, dual, left, wide, gram, sparse_hbm, dual_hbm, left_hbm, right_hbm, right, sem,
):
    copies = [
        pltpu.make_async_copy(src, dst, sem.at[i])
        for i, (src, dst) in enumerate(((sparse, sparse_hbm), (dual, dual_hbm), (left, left_hbm), (right, right_hbm)))
    ]
    for copy in copies[:3]:
        copy.start()
    right[...] = mm_high(factor_of(gram[...]), wide[...], NN)
    copies[3].start()
    for copy in copies:
        copy.wait()


def per_device(observed, sparse_init, dual_init, right_init):
    hbm = pl.BlockSpec(memory_space=pltpu.HBM)
    vmem = pl.BlockSpec(memory_space=pltpu.VMEM)
    shape = (ROWS, COLS)
    whole = jax.ShapeDtypeStruct(shape, F32)
    left_shape = jax.ShapeDtypeStruct((R, ROWS), F32)
    right_shape = jax.ShapeDtypeStruct((R, COLS), F32)
    state = pl.pallas_call(
        kernel,
        out_shape=(whole, whole, left_shape, right_shape, jax.ShapeDtypeStruct((R // 2, 2 * R), F32)),
        in_specs=[hbm] * 4,
        out_specs=(vmem,) * 5,
        scratch_shapes=[
            pltpu.VMEM((R, COLS), F32),
            pltpu.VMEM(shape, F32),
            pltpu.VMEM(shape, F32),
            pltpu.VMEM(shape, F32),
            pltpu.VMEM(shape, BF16),
            pltpu.VMEM(shape, BF16),
            pltpu.VMEM((3 * R, ROWS), BF16),
            pltpu.VMEM((2, NG, R, GB), F32),
            pltpu.VMEM((2, NG, R, GB), F32),
            pltpu.VMEM((2, NG, R, GB), F32),
            pltpu.VMEM((R, ROWS), F32),
            pltpu.VMEM((2, NP, RB, LB), F32),
            pltpu.VMEM((2, NP, RB, LB), F32),
            pltpu.VMEM((2, NP, RB, LB), F32),
            pltpu.VMEM((2, NZ, RB, 2 * R), F32),
            pltpu.VMEM((2, NX, RB, 2 * R), F32),
            pltpu.VMEM((2, NG, RB, 2 * R), F32),
            pltpu.VMEM((2, NG, R // 2, 2 * R), F32),
            pltpu.SemaphoreType.DMA((4, NY)),
            pltpu.SemaphoreType.DMA((2, 8)),
            pltpu.SemaphoreType.DMA((2, 8)),
            pltpu.SemaphoreType.DMA((2, NY)),
            pltpu.SemaphoreType.DMA((2, NY)),
        ],
        compiler_params=pltpu.CompilerParams(collective_id=0, has_side_effects=True, vmem_limit_bytes=48 << 20),
        name="pursuit",
    )(*(pltpu.with_memory_space_constraint(a, pltpu.HBM) for a in (observed, sparse_init, dual_init, right_init)))
    return pl.pallas_call(
        outputs,
        out_shape=(whole, whole, left_shape, right_shape),
        in_specs=[vmem] * 5,
        out_specs=(hbm,) * 4,
        scratch_shapes=[
            pltpu.VMEM((R, COLS), F32),
            pltpu.SemaphoreType.DMA((4,)),
        ],
        compiler_params=pltpu.CompilerParams(vmem_limit_bytes=24 << 20),
        name="outputs",
    )(*state)


def solution(mesh):
    return jax.shard_map(
        per_device,
        mesh=mesh,
        in_specs=(P("pix", "gal"), P("pix", "gal"), P("pix", "gal"), P(None, "gal")),
        out_specs=(P("pix", "gal"), P("pix", "gal"), P(None, "pix"), P(None, "gal")),
        check_vma=False,
    )
```

time: 837 us -> 75.8 us (0.09)
  waiting for transfers between devices: 448 us -> 0 us
  blocking collectives: 282 us -> 0 us
  Pallas kernels: 0 us -> 75.1 us
  other arithmetic: 48.3 us -> 0 us
  matrix products: 40.7 us -> 0 us
  between operations: 14 us -> 0.64 us
    psum x4 -> x0, waiting for transfers between devices: 448 us -> none  [the longest x2 318 us: per_device(): wide = lax.psum(partial_wide, 'pix')]
    psum x4 -> x0, blocking collectives: 282 us -> none  [the longest x2 231 us: per_device(): gram_left = lax.psum(gram_of(panel), 'pix')]
    pallas_call x0 -> x2, Pallas kernels: none -> 75.1 us  [the longest x1 70 us: per_device(): pl.pallas_call(kernel, out_shape=(whole, whole, left_shape, right_shape,...]
    another operation x20 -> x0, other arithmetic: 48.3 us -> none  [the longest x12 26.1 us: orth_with(): factor = jnp.linalg.cholesky(gram)]
    dot_general x10 -> x0, matrix products: 36.7 us -> none  [the longest x2 14.4 us: per_device(): lax.dot_general(left, wide, (((0,), (0,)), ((), ())), precision=HIGH)]
  transfers between devices with their start and end apart: 4 -> 0, of which waited for: 4 -> 0; matrix products, arithmetic and copies ran while one was open for 0% -> 0% of each run, Pallas kernels for 0% -> 0%
where the time goes in v2:
time: 75.8 us; the launch traced here: 75.7 us
  Pallas kernels  75.1 us (99%)
    pallas_call x1, Pallas kernels, per_device(): pl.pallas_call(kernel, out_shape=(whole, whole, left_shape, right_shape,...  70 us
    pallas_call x1, Pallas kernels, per_device(): pl.pallas_call(outputs, out_shape=(whole, whole, left_shape, right_shape)...  5.05 us

profile of v2, /device:TPU:1, one launch (start us, length us, event | category | flops | bytes accessed | tf_op | source)
XLA Modules:
  0.0 75.7 jit_solution(9574622304930367704)
XLA Ops:
  0.6 70.0 %pursuit.1 = (f32[1024,512]{1,0:T(8,128)S(1)}, f32[1024,512]{1,0:T(8,128)S(1)}, f32[64,1024]{1,0:T(8,128)S(1)}, f32[64,512]{1,0:T(8,128)S(1)}, f32[32,128]{1,0:T(8,128)S(1)}) custom-call(f32[1024,512]{1,0:T(8,128)} %obs_hbm.1, f32[1024,512]{1,0:T(8,128)} %sp_hbm.1, f32[1024,512]{1,0:T(8,128)} %du_hbm.1, f32[64,512]{1,0:T(8,128)} %right_hbm.1), custom_call_target="tpu_custom_call" | custom-call | tf_op jit(solution)/shard_map/pursuit/pallas_call | solution.py:383
  70.7 5.0 %outputs.1 = (f32[1024,512]{1,0:T(8,128)}, f32[1024,512]{1,0:T(8,128)}, f32[64,1024]{1,0:T(8,128)}, f32[64,512]{1,0:T(8,128)}) custom-call(f32[1024,512]{1,0:T(8,128)S(1)} %get-tuple-element.9.sparse, f32[1024,512]{1,0:T(8,128)S(1)} %get-tuple-element.10.dual, f32[64,1024]{1,0:T(8,128)S(1)} %get-tuple-element.11.left, f32[64,512]{1,0:T(8,128)S(1)} %get-tuple-element.12.wide, ...), custom_call_target="tpu_custom_call" | custom-call | tf_op jit(solution)/shard_map/outputs/pallas_call | solution.py:416

commit v3 on v2

v3 whole, which is shorter than its diff:
```python
import contextlib

import jax
import jax.numpy as jnp
from jax import lax
from jax.experimental import pallas as pl
from jax.experimental.pallas import tpu as pltpu
from jax.sharding import PartitionSpec as P

MU = 1.25
TAU = 0.6 / 1.25
INV_MU = 1.0 / MU
HIGH = lax.Precision.HIGHEST
MESH = pl.DeviceIdType.MESH
F32 = jnp.float32
BF16 = jnp.bfloat16

NY = 4
NG = 8
NZ = 8
NX = 4
NP = NZ * NX
R = 64
ROWS = 1024
COLS = 512
GB = ROWS // NG
RB = 8
LB = 128
CHUNK = ROWS // NY
ORDER = (2, 1, 3, 0)

PIX_ORDER = sorted(
    ((i, j) for i in range(NX) for j in range(NZ) if i or j), key=lambda k: -(min(k[0], NX - k[0]) + min(k[1], NZ - k[1]))
)

PEX, PRS, PAG, WRS, WAG, KG, KZ, KX, KAG, GAR = range(10)

NN = (((1,), (0,)), ((), ()))
NT = (((1,), (1,)), ((), ()))
TN = (((0,), (0,)), ((), ()))


def split(value):
    high = value.astype(BF16)
    return high, (value - high.astype(F32)).astype(BF16)


def split3(value):
    high = value.astype(BF16)
    mid, low = split(value - high.astype(F32))
    return high, mid, low


def mm(a, b, dims):
    return lax.dot_general(a, b, dims, preferred_element_type=F32)


def mm_high(a, b, dims):
    return lax.dot_general(a, b, dims, precision=HIGH, preferred_element_type=F32)


def twin_gram(value):
    high, mid, low = split3(value)
    out = mm(jnp.concatenate([high, mid, low], axis=0), jnp.concatenate([high, high, mid, mid, low, low], axis=0), NT)
    out = out[:R] + (out[R : 2 * R] + out[2 * R :])
    return out[:, : 2 * R] + (out[:, 2 * R : 4 * R] + out[:, 4 * R :])


def stacked(value):
    return jnp.concatenate(split3(value), axis=0)


def mm3(a, high, mid, low, dims):
    first = mm(a, high, dims)
    second = mm(a[: 2 * R], mid, dims)
    third = mm(a[:R], low, dims)
    return first[:R] + ((first[R : 2 * R] + second[:R]) + (first[2 * R :] + second[R:] + third))


def clip(value):
    return jnp.minimum(jnp.maximum(value, -TAU), TAU)


def solver(e00, e01, e02, e03, e11, e12, e13, e22, e23, e33):
    det = e00 * e11 - e01 * e01
    inv = 1.0 / det
    n00, n01, n11 = e11 * inv, -(e01 * inv), e00 * inv
    x00, x01 = n00 * e02 + n01 * e12, n00 * e03 + n01 * e13
    x10, x11 = n01 * e02 + n11 * e12, n01 * e03 + n11 * e13
    s00 = e22 - (e02 * x00 + e12 * x10)
    s01 = e23 - (e02 * x01 + e12 * x11)
    s11 = e33 - (e03 * x01 + e13 * x11)
    sdet = s00 * s11 - s01 * s01
    sinv = 1.0 / sdet
    m00, m01, m11 = s11 * sinv, -(s01 * sinv), s00 * sinv

    def reduce(v0, v1, v2, v3):
        return v2 - (x00 * v0 + x10 * v1), v3 - (x01 * v0 + x11 * v1)

    def solve(v0, v1, v2, v3):
        u2, u3 = reduce(v0, v1, v2, v3)
        y2, y3 = m00 * u2 + m01 * u3, m01 * u2 + m11 * u3
        y0 = (n00 * v0 + n01 * v1) - (x00 * y2 + x01 * y3)
        y1 = (n01 * v0 + n11 * v1) - (x10 * y2 + x11 * y3)
        return y0, y1, y2, y3

    def factor(v0, v1, v2, v3):
        u2, u3 = reduce(v0, v1, v2, v3)
        return (
            v0 * (1.0 / jnp.sqrt(e00)),
            (v1 - (e01 / e00) * v0) * (1.0 / jnp.sqrt(det / e00)),
            u2 * (1.0 / jnp.sqrt(s00)),
            (u3 - (s01 / s00) * u2) * (1.0 / jnp.sqrt(sdet / s00)),
        )

    return solve, factor


def inverse_factor(gram2):
    tile = (8, 128)
    lane = lax.broadcasted_iota(jnp.int32, tile, 1)
    sub = lax.broadcasted_iota(jnp.int32, tile, 0)
    tiles, out = [], []
    for b in range(8):
        eye = jnp.where(lane == sub + 8 * b, 1.0, 0.0)
        tiles.append(jnp.where(lane < R, eye, gram2[8 * b : 8 * b + 8, :]))

    def row(value, p):
        return jnp.broadcast_to(value[p : p + 1, :], tile)

    def four(e, first):
        return [e[first + p, first + q] for p in range(4) for q in range(p, 4)]

    for t in range(8):
        columns = [
            [jnp.broadcast_to(tiles[b][:, R + 8 * t + q : R + 8 * t + q + 1], tile) for q in range(8)] for b in range(t, 8)
        ]
        rows = [row(tiles[t], p) for p in range(8)]
        e = {(p, q): row(columns[0][q], p) for q in range(8) for p in range(q + 1)}
        solve, factor = solver(*four(e, 0))
        upper = rows[:4]
        y = solve(*upper)
        cross = [solve(*(e[r, q] for r in range(4))) for q in range(4, 8)]

        def less(value, p, ys):
            return value - ((e[0, p] * ys[0] + e[1, p] * ys[1]) + (e[2, p] * ys[2] + e[3, p] * ys[3]))

        late = {(p, q): less(e[p, q], p, cross[q - 4]) for q in range(4, 8) for p in range(4, q + 1)}
        lower = [less(rows[p], p, y) for p in range(4, 8)]
        solve_late, factor_late = solver(*four(late, 4))
        done = [*factor(*upper), *factor_late(*lower)]
        result = done[7]
        for p in range(6, -1, -1):
            result = jnp.where(sub == p, done[p], result)
        out.append(result)
        if t < 7:
            w = solve_late(*lower)
            full = [
                y[r] - ((cross[0][r] * w[0] + cross[1][r] * w[1]) + (cross[2][r] * w[2] + cross[3][r] * w[3]))
                for r in range(4)
            ] + list(w)
            for b in range(t + 1, 8):
                terms = [columns[b - t][q] * full[q] for q in range(8)]
                tiles[b] = tiles[b] - (
                    ((terms[0] + terms[1]) + (terms[2] + terms[3])) + ((terms[4] + terms[5]) + (terms[6] + terms[7]))
                )
    return jnp.concatenate(out, axis=0)


def product(inverse, value):
    return mm_high(inverse[:, :R], value, NN)


def factor_of(packed):
    return inverse_factor(jnp.concatenate([pltpu.roll(packed, R, 1), packed], axis=0))


def scope(name):
    return contextlib.nullcontext()


def kernel(
    obs_hbm, sp_hbm, du_hbm, right_hbm, sparse_out, dual_out, left_ref, wide_ref, gram_ref,
    right_ref, obs, work, dual, thi, tmid, tlo, lstk,
    part, pex, prs, panel, normal, wpart, wrs, wraw, kpart, kg, kz, kx, kraw, gall,
    load_sem, send_sem, recv_sem, pex_sem, near_sem, relay_sem,
):
    g = lax.axis_index("gal")
    pix = lax.axis_index("pix")
    y, core = lax.div(g, 2), lax.rem(g, 2)
    other = 1 - core
    z = lax.rem(pix, NZ)
    x = lax.div(pix, NZ)

    def gal_peer(t):
        return {"gal": t, "pix": pix}

    def z_peer(t):
        return {"gal": g, "pix": x * NZ + t}

    def x_peer(t):
        return {"gal": g, "pix": t * NZ + z}

    def pix_of(k):
        return lax.rem(x + k[0], NX) * NZ + lax.rem(z + k[1], NZ)

    def pix_peer(k):
        return {"gal": g, "pix": pix_of(k)}

    def chunk(k):
        return lax.rem(y + k, NY)

    def rows_of(k):
        return pl.ds(pl.multiple_of(chunk(k) * CHUNK, CHUNK), CHUNK)

    def loads(k):
        rows = rows_of(k)
        return [
            pltpu.make_async_copy(src.at[rows, :], dst.at[rows, :], load_sem.at[i, k])
            for i, (src, dst) in enumerate(((obs_hbm, obs), (sp_hbm, work), (du_hbm, dual)))
        ]

    load_right = pltpu.make_async_copy(right_hbm, right_ref, load_sem.at[3, 0])
    load_right.start()
    for k in ORDER:
        for copy in loads(k):
            copy.start()
    barrier = pltpu.get_barrier_semaphore()
    for k in PIX_ORDER:
        pl.semaphore_signal(barrier, inc=1, device_id=pix_peer(k), device_id_type=MESH)
    for k in range(1, NG):
        pl.semaphore_signal(barrier, inc=1, device_id=gal_peer(lax.rem(g + k, NG)), device_id_type=MESH)

    def send(it, kind, src, dst, peer, recv):
        pltpu.make_async_remote_copy(
            src_ref=src, dst_ref=dst, send_sem=send_sem.at[it, kind], recv_sem=recv,
            device_id=peer, device_id_type=MESH,
        ).start()

    def spread(it, kind, n, me, peer, src_of, dst):
        order = sorted(range(1, n), key=lambda k: -min(k, n - k))
        for k in order:
            t = lax.rem(me + k, n)
            send(it, kind, src_of(t), dst.at[it, me], peer(t), recv_sem.at[it, kind])

    def arrived(it, kind, n, dst):
        view = dst.at[it, pl.ds(0, n - 1)]
        pltpu.make_async_copy(view, view, recv_sem.at[it, kind]).wait()

    def landed(view, sem):
        pltpu.make_async_copy(view, view, sem).wait()

    def total(buf, it, n):
        acc = buf[it, 0]
        for i in range(1, n):
            acc = acc + buf[it, i]
        return acc

    def panel_chunk(it, k, r3, target):
        rows = rows_of(k)
        terms = split3(target)
        for dst, term in zip((thi, tmid, tlo), terms):
            dst[rows, :] = term
        p = mm3(r3, *terms, NT)
        first = 2 * chunk(k)
        part[it, first] = p[:, :GB]
        part[it, first + 1] = p[:, GB:]

    def to_partner(it, k):
        send(it, PEX, part.at[it, 2 * chunk(k) + other], pex.at[it, k], gal_peer(2 * y + other), pex_sem.at[it, k])

    def from_partner(it, k):
        landed(pex.at[it, k], pex_sem.at[it, k])
        d = 2 * chunk(k) + core
        part[it, d] = part[it, d] + pex[it, k]
        if k:
            send(it, PRS, part.at[it, d], prs.at[it, NY - k], gal_peer(d), recv_sem.at[it, PRS])

    with scope("load_right"):
        load_right.wait()
        r3 = stacked(right_ref[...])
    for k in ORDER:
        with scope("load"):
            for copy in loads(k):
                copy.wait()
        with scope("target"):
            rows = rows_of(k)
            c = dual[rows, :] * INV_MU
            dual[rows, :] = c
            target = obs[rows, :] - work[rows, :] + c
        with scope("panel"):
            panel_chunk(0, k, r3, target)
        if k == ORDER[0]:
            with scope("barrier"):
                pl.semaphore_wait(barrier, NG + NP - 2)
        to_partner(0, k)
        if k != ORDER[0]:
            from_partner(0, last)
        last = k
    from_partner(0, last)

    for it in range(2):
        if it == 1:
            with scope("w_gar"):
                arrived(0, GAR, NG, gall)
            with scope("chol_right"):
                inv_right = factor_of(total(gall, 0, NG))
        with scope("w_prs"):
            view = prs.at[it, pl.ds(1, NY - 1)]
            landed(view, recv_sem.at[it, PRS])
        with scope("pag_send"):
            mine = (part[it, g] + prs[it, 1]) + (prs[it, 2] + prs[it, 3])
            if it == 1:
                mine = product(inv_right, mine)
            panel[it, g] = mine
            own = panel.at[it, g]
            for k in (2, 1, 3):
                send(it, PAG, own, own, gal_peer(2 * chunk(k) + core), near_sem.at[it, NY - k])
            partner = gal_peer(2 * y + other)
            send(it, PAG, own, own, partner, near_sem.at[it, 0])
        with scope("gram_left"):
            gram = twin_gram(mine)
            for d in range(NG):
                kpart[it, d] = gram[d * RB : (d + 1) * RB]
            spread(it, KG, NG, g, gal_peer, lambda t: kpart.at[it, t], kg)
            kg[it, g] = kpart[it, g]

        def send_kz():
            with scope("w_kg"):
                arrived(it, KG, NG, kg)
            kz[it, z] = total(kg, it, NG)
            spread(it, KZ, NZ, z, z_peer, lambda t: kz.at[it, z], kz)

        raw = None

        def relay(k):
            with scope("w_relay"):
                slot = panel.at[it, 2 * chunk(k) + core]
                landed(slot, near_sem.at[it, k])
                send(it, PAG, slot, slot, partner, relay_sem.at[it, k])

        for k in (0, 1, 3, 2):
            block = 2 * chunk(k)
            rows = rows_of(k)
            with scope("w_near"):
                landed(panel.at[it, block + other], near_sem.at[it, 0] if k == 0 else relay_sem.at[it, k])
            with scope("norm"):
                p = jnp.concatenate([panel[it, block], panel[it, block + 1]], axis=1)
                normal[:, rows] = p
            with scope("raw_wide"):
                term = mm3(stacked(p), thi[rows, :], tmid[rows, :], tlo[rows, :], NN)
                raw = term if raw is None else raw + term
            if k == 0:
                relay(1)
                relay(3)
            elif k == 1:
                relay(2)
            if k == 1:
                send_kz()
        with scope("w_send"):
            for i in range(NX):
                for j in range(NZ):
                    wpart[it, i * NZ + j] = raw[j * RB : (j + 1) * RB, i * LB : (i + 1) * LB]
            for k in PIX_ORDER:
                send(it, WRS, wpart.at[it, pix_of(k)], wrs.at[it, pix], pix_peer(k), recv_sem.at[it, WRS])
            wrs[it, pix] = wpart[it, pix]

        with scope("w_kz"):
            arrived(it, KZ, NZ, kz)
        kx[it, x] = total(kz, it, NZ)
        spread(it, KX, NX, x, x_peer, lambda t: kx.at[it, x], kx)

        def finish_k():
            with scope("w_kx"):
                arrived(it, KX, NX, kx)
            kraw[it, g] = total(kx, it, NX)
            spread(it, KAG, NG, g, gal_peer, lambda t: kraw.at[it, g], kraw)

        with scope("w_wrs"):
            arrived(it, WRS, NP, wrs)
        with scope("wag_send"):
            wraw[it, pix] = total(wrs, it, NP)
            own = wraw.at[it, pix]
            for k in PIX_ORDER:
                send(it, WAG, own, own, pix_peer(k), recv_sem.at[it, WAG])
        finish_k()

        with scope("w_kag"):
            arrived(it, KAG, NG, kraw)
        with scope("chol_left"):
            inv_left = inverse_factor(jnp.concatenate([kraw[it, i] for i in range(NG)], axis=0))

        def put_left():
            with scope("left"):
                left = product(inv_left, normal[...])
                l_high, l_low = split(left)
                lstk[0:R, :] = l_high
                lstk[R : 2 * R, :] = l_high
                lstk[2 * R : 3 * R, :] = l_low
                if it == 1:
                    left_ref[...] = left

        if it == 0:
            put_left()
        with scope("w_wag"):
            arrived(it, WAG, NP, wraw)
        with scope("wide"):
            columns = [jnp.concatenate([wraw[it, i * NZ + j] for j in range(NZ)], axis=0) for i in range(NX)]
            wide = product(inv_left, jnp.concatenate(columns, axis=1))
            w_high, w_low = split(wide)
            wstk = jnp.concatenate([w_high, w_low, w_high], axis=0)
            r3 = stacked(wide)
        with scope("gram_right"):
            gram = twin_gram(wide)
            lane = lax.broadcasted_iota(jnp.int32, (R // 2, 128), 1)
            gall[it, g] = jnp.where(lane < R, gram[: R // 2], gram[R // 2 :])
            spread(it, GAR, NG, g, gal_peer, lambda t: gall.at[it, g], gall)
        if it == 1:
            put_left()
        for k in ORDER:
            with scope("update"):
                rows = rows_of(k)
                low = mm(lstk[:, rows], wstk, TN)
                c = dual[rows, :]
                if it == 0:
                    clipped = clip(obs[rows, :] + c - low)
                    dual[rows, :] = clipped
                    panel_chunk(1, k, r3, low - c + (clipped + clipped))
                    to_partner(1, k)
                    if k != ORDER[0]:
                        from_partner(1, last)
                    last = k
                else:
                    v = obs[rows, :] + c - low
                    clipped = clip(v)
                    sparse_out[rows, :] = v - clipped
                    dual_out[rows, :] = MU * clipped
        if it == 0:
            from_partner(1, last)

    wide_ref[...] = wide
    with scope("w_gar"):
        arrived(1, GAR, NG, gall)
    gram_ref[...] = total(gall, 1, NG)
    with scope("fin"):
        for it in range(2):
            for kind, n, buf in (
                (PEX, NY + 1, pex), (PRS, NY, prs), (PAG, NG, panel), (WRS, NP, wrs), (WAG, NP, wraw),
                (KG, NG, kg), (KZ, NZ, kz), (KX, NX, kx), (KAG, NG, kraw), (GAR, NG, gall),
            ):
                landed(buf.at[it, pl.ds(0, n - 1)], send_sem.at[it, kind])


def outputs(
    sparse, dual, left, wide, gram, sparse_hbm, dual_hbm, left_hbm, right_hbm, right, sem,
):
    copies = [
        pltpu.make_async_copy(src, dst, sem.at[i])
        for i, (src, dst) in enumerate(((sparse, sparse_hbm), (dual, dual_hbm), (left, left_hbm), (right, right_hbm)))
    ]
    for copy in copies[:3]:
        copy.start()
    right[...] = product(factor_of(gram[...]), wide[...])
    copies[3].start()
    for copy in copies:
        copy.wait()


def per_device(observed, sparse_init, dual_init, right_init):
    hbm = pl.BlockSpec(memory_space=pltpu.HBM)
    vmem = pl.BlockSpec(memory_space=pltpu.VMEM)
    shape = (ROWS, COLS)
    whole = jax.ShapeDtypeStruct(shape, F32)
    left_shape = jax.ShapeDtypeStruct((R, ROWS), F32)
    right_shape = jax.ShapeDtypeStruct((R, COLS), F32)
    state = pl.pallas_call(
        kernel,
        out_shape=(whole, whole, left_shape, right_shape, jax.ShapeDtypeStruct((R // 2, 2 * R), F32)),
        in_specs=[hbm] * 4,
        out_specs=(vmem,) * 5,
        scratch_shapes=[
            pltpu.VMEM((R, COLS), F32),
            pltpu.VMEM(shape, F32),
            pltpu.VMEM(shape, F32),
            pltpu.VMEM(shape, F32),
            pltpu.VMEM(shape, BF16),
            pltpu.VMEM(shape, BF16),
            pltpu.VMEM(shape, BF16),
            pltpu.VMEM((3 * R, ROWS), BF16),
            pltpu.VMEM((2, NG, R, GB), F32),
            pltpu.VMEM((2, NY, R, GB), F32),
            pltpu.VMEM((2, NY, R, GB), F32),
            pltpu.VMEM((2, NG, R, GB), F32),
            pltpu.VMEM((R, ROWS), F32),
            pltpu.VMEM((2, NP, RB, LB), F32),
            pltpu.VMEM((2, NP, RB, LB), F32),
            pltpu.VMEM((2, NP, RB, LB), F32),
            pltpu.VMEM((2, NG, RB, 2 * R), F32),
            pltpu.VMEM((2, NG, RB, 2 * R), F32),
            pltpu.VMEM((2, NZ, RB, 2 * R), F32),
            pltpu.VMEM((2, NX, RB, 2 * R), F32),
            pltpu.VMEM((2, NG, RB, 2 * R), F32),
            pltpu.VMEM((2, NG, R // 2, 2 * R), F32),
            pltpu.SemaphoreType.DMA((4, NY)),
            pltpu.SemaphoreType.DMA((2, 10)),
            pltpu.SemaphoreType.DMA((2, 10)),
            pltpu.SemaphoreType.DMA((2, NY)),
            pltpu.SemaphoreType.DMA((2, NY)),
            pltpu.SemaphoreType.DMA((2, NY)),
        ],
        compiler_params=pltpu.CompilerParams(collective_id=0, has_side_effects=True, vmem_limit_bytes=48 << 20),
        name="pursuit",
    )(*(pltpu.with_memory_space_constraint(a, pltpu.HBM) for a in (observed, sparse_init, dual_init, right_init)))
    return pl.pallas_call(
        outputs,
        out_shape=(whole, whole, left_shape, right_shape),
        in_specs=[vmem] * 5,
        out_specs=(hbm,) * 4,
        scratch_shapes=[
            pltpu.VMEM((R, COLS), F32),
            pltpu.SemaphoreType.DMA((4,)),
        ],
        compiler_params=pltpu.CompilerParams(vmem_limit_bytes=24 << 20),
        name="outputs",
    )(*state)


def solution(mesh):
    return jax.shard_map(
        per_device,
        mesh=mesh,
        in_specs=(P("pix", "gal"), P("pix", "gal"), P("pix", "gal"), P(None, "gal")),
        out_specs=(P("pix", "gal"), P("pix", "gal"), P(None, "pix"), P(None, "gal")),
        check_vma=False,
    )
```

time: 75.8 us -> 71.3 us (0.941)
  Pallas kernels: 75.1 us -> 70.6 us
    pallas_call x1, Pallas kernels: 70 us -> 66.2 us  [per_device(): pl.pallas_call(kernel, out_shape=(whole, whole, left_shape, right_shape,...]
where the time goes in v3:
time: 71.3 us; the launch traced here: 71.2 us
  Pallas kernels  70.6 us (99%)
    pallas_call x1, Pallas kernels, per_device(): pl.pallas_call(kernel, out_shape=(whole, whole, left_shape, right_shape,...  66.2 us
    pallas_call x1, Pallas kernels, per_device(): pl.pallas_call(outputs, out_shape=(whole, whole, left_shape, right_shape)...  4.31 us

profile of v3, /device:TPU:1, one launch (start us, length us, event | category | flops | bytes accessed | tf_op | source)
XLA Modules:
  0.0 71.2 jit_solution(3904113911599321158)
XLA Ops:
  0.6 66.2 %pursuit.1 = (f32[1024,512]{1,0:T(8,128)S(1)}, f32[1024,512]{1,0:T(8,128)S(1)}, f32[64,1024]{1,0:T(8,128)S(1)}, f32[64,512]{1,0:T(8,128)S(1)}, f32[32,128]{1,0:T(8,128)S(1)}) custom-call(f32[1024,512]{1,0:T(8,128)} %obs_hbm.1, f32[1024,512]{1,0:T(8,128)} %sp_hbm.1, f32[1024,512]{1,0:T(8,128)} %du_hbm.1, f32[64,512]{1,0:T(8,128)} %right_hbm.1), custom_call_target="tpu_custom_call" | custom-call | tf_op jit(solution)/shard_map/pursuit/pallas_call | solution.py:476
  66.9 4.3 %outputs.1 = (f32[1024,512]{1,0:T(8,128)}, f32[1024,512]{1,0:T(8,128)}, f32[64,1024]{1,0:T(8,128)}, f32[64,512]{1,0:T(8,128)}) custom-call(f32[1024,512]{1,0:T(8,128)S(1)} %get-tuple-element.9.sparse, f32[1024,512]{1,0:T(8,128)S(1)} %get-tuple-element.10.dual, f32[64,1024]{1,0:T(8,128)S(1)} %get-tuple-element.11.left, f32[64,512]{1,0:T(8,128)S(1)} %get-tuple-element.12.wide, ...), custom_call_target="tpu_custom_call" | custom-call | tf_op jit(solution)/shard_map/outputs/pallas_call | solution.py:514

commit v4 on v3

--- a/solution.py
+++ b/solution.py
@@ -120,6 +120,7 @@
     tile = (8, 128)
     lane = lax.broadcasted_iota(jnp.int32, tile, 1)
     sub = lax.broadcasted_iota(jnp.int32, tile, 0)
+    zero = jnp.minimum(jnp.abs(gram2[:8, :]), 0.0)
     tiles, out = [], []
     for b in range(8):
         eye = jnp.where(lane == sub + 8 * b, 1.0, 0.0)
@@ -136,7 +137,11 @@
             [jnp.broadcast_to(tiles[b][:, R + 8 * t + q : R + 8 * t + q + 1], tile) for q in range(8)] for b in range(t, 8)
         ]
         rows = [row(tiles[t], p) for p in range(8)]
-        e = {(p, q): row(columns[0][q], p) for q in range(8) for p in range(q + 1)}
+        e = {}
+        for q in range(8):
+            spread_column = columns[0][q] + zero
+            for p in range(q + 1):
+                e[p, q] = row(spread_column, p)
         solve, factor = solver(*four(e, 0))
         upper = rows[:4]
         y = solve(*upper)
@@ -351,11 +356,9 @@
                 term = mm3(stacked(p), thi[rows, :], tmid[rows, :], tlo[rows, :], NN)
                 raw = term if raw is None else raw + term
             if k == 0:
-                relay(1)
-                relay(3)
-            elif k == 1:
-                relay(2)
-            if k == 1:
+                for kk in (1, 3, 2):
+                    relay(kk)
+            if k == 3:
                 send_kz()
         with scope("w_send"):
             for i in range(NX):

time: 71.3 us -> 69.5 us (0.975)
  Pallas kernels: 70.6 us -> 68.8 us
    pallas_call x1, Pallas kernels: 4.31 us -> 2.63 us  [per_device(): pl.pallas_call(outputs, out_shape=(whole, whole, left_shape, right_shape)...]
where the time goes in v4:
time: 69.5 us; the launch traced here: 69.4 us
  Pallas kernels  68.8 us (99%)
    pallas_call x1, Pallas kernels, per_device(): pl.pallas_call(kernel, out_shape=(whole, whole, left_shape, right_shape,...  66.2 us
    pallas_call x1, Pallas kernels, per_device(): pl.pallas_call(outputs, out_shape=(whole, whole, left_shape, right_shape)...  2.63 us

profile of v4, /device:TPU:1, one launch (start us, length us, event | category | flops | bytes accessed | tf_op | source)
XLA Modules:
  0.0 69.4 jit_solution(5197975848559934796)
XLA Ops:
  0.6 66.2 %pursuit.1 = (f32[1024,512]{1,0:T(8,128)S(1)}, f32[1024,512]{1,0:T(8,128)S(1)}, f32[64,1024]{1,0:T(8,128)S(1)}, f32[64,512]{1,0:T(8,128)S(1)}, f32[32,128]{1,0:T(8,128)S(1)}) custom-call(f32[1024,512]{1,0:T(8,128)} %obs_hbm.1, f32[1024,512]{1,0:T(8,128)} %sp_hbm.1, f32[1024,512]{1,0:T(8,128)} %du_hbm.1, f32[64,512]{1,0:T(8,128)} %right_hbm.1), custom_call_target="tpu_custom_call" | custom-call | tf_op jit(solution)/shard_map/pursuit/pallas_call | solution.py:479
  66.8 2.6 %outputs.1 = (f32[1024,512]{1,0:T(8,128)}, f32[1024,512]{1,0:T(8,128)}, f32[64,1024]{1,0:T(8,128)}, f32[64,512]{1,0:T(8,128)}) custom-call(f32[1024,512]{1,0:T(8,128)S(1)} %get-tuple-element.9.sparse, f32[1024,512]{1,0:T(8,128)S(1)} %get-tuple-element.10.dual, f32[64,1024]{1,0:T(8,128)S(1)} %get-tuple-element.11.left, f32[64,512]{1,0:T(8,128)S(1)} %get-tuple-element.12.wide, ...), custom_call_target="tpu_custom_call" | custom-call | tf_op jit(solution)/shard_map/outputs/pallas_call | solution.py:517

commit v5 on v4

--- a/solution.py
+++ b/solution.py
@@ -302,7 +302,6 @@
         if k != ORDER[0]:
             from_partner(0, last)
         last = k
-    from_partner(0, last)
 
     for it in range(2):
         if it == 1:
@@ -310,6 +309,7 @@
                 arrived(0, GAR, NG, gall)
             with scope("chol_right"):
                 inv_right = factor_of(total(gall, 0, NG))
+        from_partner(it, last)
         with scope("w_prs"):
             view = prs.at[it, pl.ds(1, NY - 1)]
             landed(view, recv_sem.at[it, PRS])
@@ -438,8 +438,6 @@
                     clipped = clip(v)
                     sparse_out[rows, :] = v - clipped
                     dual_out[rows, :] = MU * clipped
-        if it == 0:
-            from_partner(1, last)
 
     wide_ref[...] = wide
     with scope("w_gar"):

time: 69.5 us -> 69.5 us (level)
  no operation moved by 1% of the time
where the time goes in v5:
time: 69.5 us; the launch traced here: 69.4 us
  Pallas kernels  68.8 us (99%)
    pallas_call x1, Pallas kernels, per_device(): pl.pallas_call(kernel, out_shape=(whole, whole, left_shape, right_shape,...  66.2 us
    pallas_call x1, Pallas kernels, per_device(): pl.pallas_call(outputs, out_shape=(whole, whole, left_shape, right_shape)...  2.63 us

profile of v5, /device:TPU:1, one launch (start us, length us, event | category | flops | bytes accessed | tf_op | source)
XLA Modules:
  0.0 69.4 jit_solution(4678579797876746166)
XLA Ops:
  0.6 66.2 %pursuit.1 = (f32[1024,512]{1,0:T(8,128)S(1)}, f32[1024,512]{1,0:T(8,128)S(1)}, f32[64,1024]{1,0:T(8,128)S(1)}, f32[64,512]{1,0:T(8,128)S(1)}, f32[32,128]{1,0:T(8,128)S(1)}) custom-call(f32[1024,512]{1,0:T(8,128)} %obs_hbm.1, f32[1024,512]{1,0:T(8,128)} %sp_hbm.1, f32[1024,512]{1,0:T(8,128)} %du_hbm.1, f32[64,512]{1,0:T(8,128)} %right_hbm.1), custom_call_target="tpu_custom_call" | custom-call | tf_op jit(solution)/shard_map/pursuit/pallas_call | solution.py:477
  66.8 2.6 %outputs.1 = (f32[1024,512]{1,0:T(8,128)}, f32[1024,512]{1,0:T(8,128)}, f32[64,1024]{1,0:T(8,128)}, f32[64,512]{1,0:T(8,128)}) custom-call(f32[1024,512]{1,0:T(8,128)S(1)} %get-tuple-element.9.sparse, f32[1024,512]{1,0:T(8,128)S(1)} %get-tuple-element.10.dual, f32[64,1024]{1,0:T(8,128)S(1)} %get-tuple-element.11.left, f32[64,512]{1,0:T(8,128)S(1)} %get-tuple-element.12.wide, ...), custom_call_target="tpu_custom_call" | custom-call | tf_op jit(solution)/shard_map/outputs/pallas_call | solution.py:515
